TPU v7x, 512 devices: a whole 4x8x8 slice. The times are simulated.
512 devices in a mesh: row: 16 (over y, core), col: 32 (over z, x).
Axes of the slice: x: 4, y: 8, z: 8, core: 2. Of those that a mesh axis runs over, the one named last changes fastest.
Arguments:
- surface: float32 [2, 1024, 4096], P(None, 'row', 'col'), may hold values from -0.5 to 0.5
- u_face: float32 [2, 1024, 4096], P(None, 'row', 'col'), may hold values from -3 to 3
- v_face: float32 [2, 1024, 4096], P(None, 'row', 'col'), may hold values from -3 to 3
- bed_depth: float32 [1024, 4096], P('row', 'col'), may hold values from 1 to 10
- wet_mask: int32 [2, 1024, 4096], P(None, 'row', 'col'), may hold values 0 or 1
- rainfall: float32 [2, 1024, 4096], P(None, 'row', 'col'), may hold values from 0.05 to 0.5
Outputs:
- new_surface: float32 [2, 1024, 4096], P(None, 'row', 'col')
- new_u: float32 [2, 1024, 4096], P(None, 'row', 'col')
- new_v: float32 [2, 1024, 4096], P(None, 'row', 'col')
All inputs are finite; a program needn't handle non-finite values. No bound on the sum of `wet_mask` on one device may be relied on, other than what follows from the above.
Results may differ from a plain program's by a relative error of at most 0.0003.
Values sent between devices are 32-bit elements; how exact they have to be, the bound alone decides.
A program may use at most 64 MiB of HBM per device.

v0:
```python
import jax
import jax.numpy as jnp
from jax import lax
from jax.sharding import PartitionSpec as P

ITERS = 3
DTDX = 0.5
FRIC = 0.05
G1 = 4.0
CK = DTDX * G1


def extended(cells, sides, width):
    for axis, dim in sides:
        count = lax.axis_size(axis)
        ends = count - 1
        head = lax.slice_in_dim(cells, 0, width, axis=dim)
        tail = lax.slice_in_dim(cells, cells.shape[dim] - width, cells.shape[dim], axis=dim)
        cells = jnp.concatenate(
            [
                lax.ppermute(tail, axis, [(i, (i + 1) % count) for i in range(ends)]),
                cells,
                lax.ppermute(head, axis, [((i + 1) % count, i) for i in range(ends)]),
            ],
            axis=dim,
        )
    return cells


def passed_along(block, axis, distance):
    devices = range(lax.axis_size(axis))
    route = [(i - distance, i) for i in devices if i - distance in devices]
    return lax.ppermute(block, axis, route)


def explicit(eta2, u2, v2, dep2, wet2, ny, nx):

    def view(a, dy, dx):
        return a[:, 1 + dy : 3 + dy + ny, 1 + dx : 3 + dx + nx]

    h_here = view(eta2, 0, 0) + view(dep2, 0, 0)
    h_east = view(eta2, 0, 1) + view(dep2, 0, 1)
    h_north = view(eta2, 1, 0) + view(dep2, 1, 0)
    wet_x = view(wet2, 0, 0) * view(wet2, 0, 1)
    wet_y = view(wet2, 0, 0) * view(wet2, 1, 0)
    depth_x = 0.5 * (h_here + h_east)
    depth_y = 0.5 * (h_here + h_north)
    u_here = view(u2, 0, 0)
    v_here = view(v2, 0, 0)
    v_mean = 0.25 * (v_here + view(v2, 0, 1) + view(v2, -1, 0) + view(v2, -1, 1))
    u_mean = 0.25 * (u_here + view(u2, 0, -1) + view(u2, 1, 0) + view(u2, 1, -1))
    adv_u = jnp.where(
        u_here > 0, u_here * (u_here - view(u2, 0, -1)), u_here * (view(u2, 0, 1) - u_here)
    )
    adv_u = adv_u + jnp.where(
        v_mean > 0, v_mean * (u_here - view(u2, -1, 0)), v_mean * (view(u2, 1, 0) - u_here)
    )
    adv_v = jnp.where(
        v_here > 0, v_here * (v_here - view(v2, -1, 0)), v_here * (view(v2, 1, 0) - v_here)
    )
    adv_v = adv_v + jnp.where(
        u_mean > 0, u_mean * (v_here - view(v2, 0, -1)), u_mean * (view(v2, 0, 1) - v_here)
    )
    u_star = wet_x * (u_here - DTDX * adv_u) / (1.0 + FRIC * jnp.abs(u_here))
    v_star = wet_y * (v_here - DTDX * adv_v) / (1.0 + FRIC * jnp.abs(v_here))
    return (
        u_star,
        v_star,
        wet_x,
        wet_y,
        CK * depth_x * wet_x,
        CK * depth_y * wet_y,
        depth_x * u_star,
        depth_y * v_star,
    )


def inner(a):
    return a[:, 1:-1, 1:-1]


def right_side(eta, rain, flux_x, flux_y):
    div = inner(flux_x) - flux_x[:, 1:-1, :-2] + (inner(flux_y) - flux_y[:, :-2, 1:-1])
    return eta + rain - DTDX * div


def operate(e_pad, coef_x, coef_y):
    e_mid = inner(e_pad)
    out = (
        e_mid
        + inner(coef_x) * (e_mid - e_pad[:, 1:-1, 2:])
        + coef_x[:, 1:-1, :-2] * (e_mid - e_pad[:, 1:-1, :-2])
    )
    return (
        out
        + inner(coef_y) * (e_mid - e_pad[:, 2:, 1:-1])
        + coef_y[:, :-2, 1:-1] * (e_mid - e_pad[:, :-2, 1:-1])
    )


def field_pad(field):
    return extended(field, (("row", 1), ("col", 2)), 1)


def squares(residual):
    return lax.psum(jnp.sum(residual * residual, axis=(1, 2)), ("row", "col"))


def spread(values):
    return values[:, None, None]


def body(surface, u_face, v_face, bed_depth, wet_mask, rainfall):
    rows = surface.shape[1]
    cols = surface.shape[2]
    stacked = jnp.stack(
        [
            surface,
            u_face,
            v_face,
            jnp.broadcast_to(bed_depth[None], surface.shape),
            wet_mask.astype(jnp.float32),
        ]
    )
    padded = extended(stacked, (("row", 2), ("col", 3)), 2)
    u_star, v_star, wet_x, wet_y, coef_x, coef_y, flux_x, flux_y = explicit(
        padded[0], padded[1], padded[2], padded[3], padded[4], rows, cols
    )
    rhs = right_side(surface, rainfall, flux_x, flux_y)
    start_pad = padded[0][:, 1:-1, 1:-1]
    solution = surface
    residual = rhs - operate(start_pad, coef_x, coef_y)
    direction = residual
    norm_now = squares(residual)
    for step in range(ITERS):
        direction_pad = field_pad(direction)
        image = operate(direction_pad, coef_x, coef_y)
        alpha = norm_now / lax.psum(jnp.sum(direction * image, axis=(1, 2)), ("row", "col"))
        solution = solution + spread(alpha) * direction
        residual = residual - spread(alpha) * image
        norm_next = squares(residual)
        direction = residual + spread(norm_next / norm_now) * direction
        norm_now = norm_next
    east_col = passed_along(solution[:, :, :1], "col", -1)
    north_row = passed_along(solution[:, :1, :], "row", -1)
    east_field = jnp.concatenate([solution[:, :, 1:], east_col], axis=2)
    north_field = jnp.concatenate([solution[:, 1:, :], north_row], axis=1)
    new_u = inner(u_star) - G1 * inner(wet_x) * (east_field - solution)
    new_v = inner(v_star) - G1 * inner(wet_y) * (north_field - solution)
    return (solution, new_u, new_v)


def solution(mesh):
    in_specs = (
        P(None, "row", "col"),
        P(None, "row", "col"),
        P(None, "row", "col"),
        P("row", "col"),
        P(None, "row", "col"),
        P(None, "row", "col"),
    )
    out_specs = (P(None, "row", "col"), P(None, "row", "col"), P(None, "row", "col"))
    return jax.shard_map(body, mesh=mesh, in_specs=in_specs, out_specs=out_specs, check_vma=False)
```

profile of v0, /device:TPU:14, one launch (start us, length us, event | category | flops | bytes accessed | tf_op | source)
XLA Modules:
  0.0 589.8 jit_solution(1745346275453686401)
XLA Ops:
  0.6 0.9 bitcast_dynamic-update-slice_fusion.3
  1.5 0.8 copy-done.4
  2.4 0.7 copy-done.6
  3.1 0.8 copy-done.5
  4.0 1.9 collective-permute-start
  5.9 3.6 collective-permute-start.1
  9.6 1.4 collective-permute-done.1
  11.1 4.2 collective-permute-start.2
  15.3 1.9 collective-permute-start.3
  17.3 6.6 %collective-permute-done.2 = f32[5,2,68,2]{3,2,1,0:T(8,128)S(1)} collective-permute-done((f32[5,2,68,2]{3,2,1,0:T(8,128)S(1)}, f32[5,2,68,2]{3,2,1,0:T(8,128)S(1)}, u32[]{:S(2)}, u32[]{:S(2)}) %collective-permute-start.2) | collective-permute-done | bytes 5472 | tf_op jit(solution)/shard_map/ppermute | solution.py:21
  23.8 6.6 %collective-permute-done.3 = f32[5,2,68,2]{3,2,1,0:T(8,128)S(1)} collective-permute-done((f32[5,2,68,2]{3,2,1,0:T(8,128)S(1)}, f32[5,2,68,2]{3,2,1,0:T(8,128)S(1)}, u32[]{:S(2)}, u32[]{:S(2)}) %collective-permute-start.3) | collective-permute-done | bytes 5472 | tf_op jit(solution)/shard_map/ppermute | solution.py:23
  30.5 0.4 pad_maximum_fusion
  30.9 0.4 fusion.76
  31.4 0.4 multiply_multiply_fusion.1
  31.8 0.3 multiply_multiply_fusion
  32.1 0.5 copy-done.1
  32.9 1.9 collective-permute-start.5
  34.8 2.4 collective-permute-start.4
  37.3 2.5 collective-permute-done.4
  39.8 1.9 collective-permute-start.6
  41.7 6.0 %collective-permute-start.7 = (f32[2,66,1]{2,1,0:T(8,128)S(1)}, f32[2,66,1]{2,1,0:T(8,128)S(1)}, u32[]{:S(2)}, u32[]{:S(2)}) collective-permute-start(f32[2,66,1]{2,1,0:T(8,128)S(1)} %get-tuple-element.39), channel_id=1, source_target_pairs={{0,1},{1,2},{2,3},{3,4},{4,5},{5,6},{6,7},{7,8},{8,9},{9,10},{10,1... | collective-permute-start | bytes 1592 | tf_op jit(solution)/shard_map/ppermute | solution.py:21
  47.8 0.4 collective-permute-done.6
  48.2 1.6 collective-permute-done.7
  49.7 0.3 multiply_reduce_fusion.3
  50.0 105.9 %all-reduce = (f32[2]{0:T(128)S(1)}, f32[2]{0:T(128)S(1)}) all-reduce(f32[2]{0:T(128)S(1)} %get-tuple-element.4, f32[2]{0:T(128)S(1)} %get-tuple-element.3), channel_id=1, replica_groups=mesh['row'=16,'col'=32] {'row','col'}, use_global_device_ids=true, to_apply=%region_1.2 | all-reduce | flops 4 | bytes 32 | tf_op jit(solution)/shard_map/psum | solution.py:106
  156.1 94.5 %psum.44 = f32[2]{0:T(128)S(1)} all-reduce(f32[2]{0:T(128)S(1)} %get-tuple-element.9), channel_id=1, replica_groups=mesh['row'=16,'col'=32] {'row','col'}, use_global_device_ids=true, to_apply=%region_5.6 | all-reduce | flops 2 | bytes 16 | tf_op jit(solution)/shard_map/psum | solution.py:106
  250.7 1.9 collective-permute-start.9
  252.6 2.4 collective-permute-start.8
  255.1 2.5 collective-permute-done.8
  257.6 2.2 collective-permute-start.10
  259.8 5.8 collective-permute-start.11
  265.6 0.4 collective-permute-done.10
  266.0 1.6 collective-permute-done.11
  267.6 0.3 multiply_reduce_fusion.1
  267.8 99.5 %psum.45 = f32[2]{0:T(128)S(1)} all-reduce(f32[2]{0:T(128)S(1)} %get-tuple-element.7), channel_id=1, replica_groups=mesh['row'=16,'col'=32] {'row','col'}, use_global_device_ids=true, to_apply=%region_7.8 | all-reduce | flops 2 | bytes 16 | tf_op jit(solution)/shard_map/psum | solution.py:138
  367.5 94.4 %psum.46 = f32[2]{0:T(128)S(1)} all-reduce(f32[2]{0:T(128)S(1)} %multiply_reduce_fusion), channel_id=1, replica_groups=mesh['row'=16,'col'=32] {'row','col'}, use_global_device_ids=true, to_apply=%region_9.10 | all-reduce | flops 2 | bytes 16 | tf_op jit(solution)/shard_map/psum | solution.py:106
  461.9 1.9 collective-permute-start.13
  463.9 2.4 collective-permute-start.12
  466.3 2.5 collective-permute-done.12
  468.8 2.2 collective-permute-start.14
  471.1 5.7 collective-permute-start.15
  476.8 0.4 collective-permute-done.14
  477.2 1.6 collective-permute-done.15
  479.0 99.4 %psum.47 = f32[2]{0:T(128)S(1)} all-reduce(f32[2]{0:T(128)S(1)} %fusion.28), channel_id=1, replica_groups=mesh['row'=16,'col'=32] {'row','col'}, use_global_device_ids=true, to_apply=%region_11.12 | all-reduce | flops 2 | bytes 16 | tf_op jit(solution)/shard_map/psum | solution.py:138
  578.5 1.9 collective-permute-start.17
  580.5 1.9 collective-permute-start.16
  582.5 6.5 %collective-permute-done.16 = f32[2,64,1]{2,1,0:T(8,128)S(1)} collective-permute-done((f32[2,64,1]{2,1,0:T(8,128)S(1)}, f32[2,64,1]{2,1,0:T(8,128)S(1)}, u32[]{:S(2)}, u32[]{:S(2)}) %collective-permute-start.16) | collective-permute-done | bytes 544 | tf_op jit(solution)/shard_map/ppermute | solution.py:33
  589.0 0.8 fusion.21
  (47 shorter events, 1.9 us)
Async XLA Ops:
  0.6 0.9 copy-start.3
  1.5 0.8 copy-start.4
  2.4 0.8 copy-start.6
  3.1 0.8 copy-start.5
  4.0 5.6 collective-permute-start
  5.9 5.0 collective-permute-start.1
  11.1 12.7 %collective-permute-start.2 = (f32[5,2,68,2]{3,2,1,0:T(8,128)S(1)}, f32[5,2,68,2]{3,2,1,0:T(8,128)S(1)}, u32[]{:S(2)}, u32[]{:S(2)}) collective-permute-start(f32[5,2,68,2]{3,2,1,0:T(8,128)S(1)} %get-tuple-element.30), channel_id=1, source_target_pairs={{0,1},{1,2},{2,3},{3,4},{4,5},{5,6},{6,7},{7,8},{8,9},{9,10},{10,1... | collective-permute-start | bytes 16328 | tf_op jit(solution)/shard_map/ppermute | solution.py:21
  15.3 15.1 %collective-permute-start.3 = (f32[5,2,68,2]{3,2,1,0:T(8,128)S(1)}, f32[5,2,68,2]{3,2,1,0:T(8,128)S(1)}, u32[]{:S(2)}, u32[]{:S(2)}) collective-permute-start(f32[5,2,68,2]{3,2,1,0:T(8,128)S(1)} %get-tuple-element.31), channel_id=1, source_target_pairs={{1,0},{2,1},{3,2},{4,3},{5,4},{6,5},{7,6},{8,7},{9,8},{10,9},{11,1... | collective-permute-start | bytes 16328 | tf_op jit(solution)/shard_map/ppermute | solution.py:23
  31.8 0.8 copy-start.1
  31.8 0.9 copy-start.2
  32.9 4.3 collective-permute-start.5
  34.8 4.9 collective-permute-start.4
  39.8 8.4 %collective-permute-start.6 = (f32[2,66,1]{2,1,0:T(8,128)S(1)}, f32[2,66,1]{2,1,0:T(8,128)S(1)}, u32[]{:S(2)}, u32[]{:S(2)}) collective-permute-start(f32[2,66,1]{2,1,0:T(8,128)S(1)} %get-tuple-element.38), channel_id=1, source_target_pairs={{1,0},{2,1},{3,2},{4,3},{5,4},{6,5},{7,6},{8,7},{9,8},{10,9},{11,1... | collective-permute-start | bytes 1592 | tf_op jit(solution)/shard_map/ppermute | solution.py:23
  41.7 8.0 %collective-permute-start.7 = (f32[2,66,1]{2,1,0:T(8,128)S(1)}, f32[2,66,1]{2,1,0:T(8,128)S(1)}, u32[]{:S(2)}, u32[]{:S(2)}) collective-permute-start(f32[2,66,1]{2,1,0:T(8,128)S(1)} %get-tuple-element.39), channel_id=1, source_target_pairs={{0,1},{1,2},{2,3},{3,4},{4,5},{5,6},{6,7},{7,8},{8,9},{9,10},{10,1... | collective-permute-start | bytes 1592 | tf_op jit(solution)/shard_map/ppermute | solution.py:21
  250.7 4.3 collective-permute-start.9
  252.6 4.9 collective-permute-start.8
  257.6 8.4 %collective-permute-start.10 = (f32[2,66,1]{2,1,0:T(8,128)S(1)}, f32[2,66,1]{2,1,0:T(8,128)S(1)}, u32[]{:S(2)}, u32[]{:S(2)}) collective-permute-start(f32[2,66,1]{2,1,0:T(8,128)S(1)} %get-tuple-element.36), channel_id=1, source_target_pairs={{1,0},{2,1},{3,2},{4,3},{5,4},{6,5},{7,6},{8,7},{9,8},{10,9},{11,1... | collective-permute-start | bytes 1592 | tf_op jit(solution)/shard_map/ppermute | solution.py:23
  259.8 7.7 %collective-permute-start.11 = (f32[2,66,1]{2,1,0:T(8,128)S(1)}, f32[2,66,1]{2,1,0:T(8,128)S(1)}, u32[]{:S(2)}, u32[]{:S(2)}) collective-permute-start(f32[2,66,1]{2,1,0:T(8,128)S(1)} %get-tuple-element.37), channel_id=1, source_target_pairs={{0,1},{1,2},{2,3},{3,4},{4,5},{5,6},{6,7},{7,8},{8,9},{9,10},{10,1... | collective-permute-start | bytes 1592 | tf_op jit(solution)/shard_map/ppermute | solution.py:21
  461.9 4.3 collective-permute-start.13
  463.9 4.9 collective-permute-start.12
  468.8 8.4 %collective-permute-start.14 = (f32[2,66,1]{2,1,0:T(8,128)S(1)}, f32[2,66,1]{2,1,0:T(8,128)S(1)}, u32[]{:S(2)}, u32[]{:S(2)}) collective-permute-start(f32[2,66,1]{2,1,0:T(8,128)S(1)} %get-tuple-element.34), channel_id=1, source_target_pairs={{1,0},{2,1},{3,2},{4,3},{5,4},{6,5},{7,6},{8,7},{9,8},{10,9},{11,1... | collective-permute-start | bytes 1592 | tf_op jit(solution)/shard_map/ppermute | solution.py:23
  471.1 7.7 %collective-permute-start.15 = (f32[2,66,1]{2,1,0:T(8,128)S(1)}, f32[2,66,1]{2,1,0:T(8,128)S(1)}, u32[]{:S(2)}, u32[]{:S(2)}) collective-permute-start(f32[2,66,1]{2,1,0:T(8,128)S(1)} %get-tuple-element.35), channel_id=1, source_target_pairs={{0,1},{1,2},{2,3},{3,4},{4,5},{5,6},{6,7},{7,8},{8,9},{9,10},{10,1... | collective-permute-start | bytes 1592 | tf_op jit(solution)/shard_map/ppermute | solution.py:21
  578.5 10.5 %copy-start = (f32[2,64,128]{2,1,0:T(8,128)}, f32[2,64,128]{2,1,0:T(8,128)S(1)}, u32[]{:S(2)}) copy-start(f32[2,64,128]{2,1,0:T(8,128)S(1)} %multiply_add_fusion) | copy-start | bytes 196612
  578.5 10.4 %collective-permute-start.17 = (f32[2,1,128]{2,1,0:T(1,128)S(1)}, f32[2,1,128]{2,1,0:T(1,128)S(1)}, u32[]{:S(2)}, u32[]{:S(2)}) collective-permute-start(f32[2,1,128]{2,1,0:T(1,128)S(1)} %slice.398), channel_id=1, source_target_pairs={{32,0},{64,32},{96,64},{128,96},{160,128},{192,160},{224,192},{256... | collective-permute-start | bytes 3080 | tf_op jit(solution)/shard_map/ppermute | solution.py:33
  580.5 8.5 %collective-permute-start.16 = (f32[2,64,1]{2,1,0:T(8,128)S(1)}, f32[2,64,1]{2,1,0:T(8,128)S(1)}, u32[]{:S(2)}, u32[]{:S(2)}) collective-permute-start(f32[2,64,1]{2,1,0:T(8,128)S(1)} %bitcast.19), channel_id=1, source_target_pairs={{1,0},{2,1},{3,2},{4,3},{5,4},{6,5},{7,6},{8,7},{9,8},{10,9},{11,1... | collective-permute-start | bytes 1544 | tf_op jit(solution)/shard_map/ppermute | solution.py:33
where the time goes:
time: 591 us; the launch traced here: 590 us
  blocking collectives  494 us (84%)
  starting transfers between devices  52.3 us (9%)
  waiting for transfers between devices  34.3 us (6%)
    psum x3, blocking collectives, squares(): return lax.psum(jnp.sum(residual * residual, axis=(1, 2)), ('row', 'col'))  295 us
    psum x2, blocking collectives, body(): lax.psum(jnp.sum(direction * image, axis=(1, 2)), ('row', 'col'))  199 us
    ppermute x8, starting transfers between devices, extended(): lax.ppermute(tail, axis, [(i, (i + 1) % count) for i in range(ends)])  30.9 us
    ppermute x8, waiting for transfers between devices, extended(): lax.ppermute(tail, axis, [(i, (i + 1) % count) for i in range(ends)])  18.7 us
    ppermute x8, starting transfers between devices, extended(): lax.ppermute(head, axis, [((i + 1) % count, i) for i in range(ends)])  17.6 us
  transfers between devices with their start and end apart: 18, of which 13 were waited for; matrix products, arithmetic and copies ran while one was open for 0% of the time, Pallas kernels for 0%

commit v1 on v0

--- a/solution.py
+++ b/solution.py
@@ -103,7 +103,9 @@
 
 
 def squares(residual):
-    return lax.psum(jnp.sum(residual * residual, axis=(1, 2)), ("row", "col"))
+    return jnp.sum(
+        lax.all_gather(jnp.sum(residual * residual, axis=(1, 2)), ("row", "col")), axis=0
+    )
 
 
 def spread(values):

time: 591 us -> 596 us (level)
    unnamed x0 -> x3, blocking collectives: none -> 295 us
    psum x3 -> x0, blocking collectives: 295 us -> none  [squares(): return lax.psum(jnp.sum(residual * residual, axis=(1, 2)), ('row', 'col'))]
    ppermute x8, waiting for transfers between devices: 18.7 us -> 10.7 us  [extended(): lax.ppermute(tail, axis, [(i, (i + 1) % count) for i in range(ends)])]
where the time goes in v1:
time: 596 us; the launch traced here: 595 us
  blocking collectives  496 us (83%)
  starting transfers between devices  56.1 us (9%)
  waiting for transfers between devices  31.4 us (5%)
    unnamed x3, blocking collectives  295 us
    psum x2, blocking collectives, body(): lax.psum(jnp.sum(direction * image, axis=(1, 2)), ('row', 'col'))  201 us
    ppermute x8, starting transfers between devices, extended(): lax.ppermute(tail, axis, [(i, (i + 1) % count) for i in range(ends)])  29.6 us
    ppermute x8, starting transfers between devices, extended(): lax.ppermute(head, axis, [((i + 1) % count, i) for i in range(ends)])  22.6 us
    ppermute x8, waiting for transfers between devices, extended(): lax.ppermute(head, axis, [((i + 1) % count, i) for i in range(ends)])  14.2 us
  transfers between devices with their start and end apart: 18, of which 13 were waited for; matrix products, arithmetic and copies ran while one was open for 0% of the time, Pallas kernels for 0%

profile of v1, /device:TPU:14, one launch (start us, length us, event | category | flops | bytes accessed | tf_op | source)
XLA Modules:
  0.0 594.7 jit_solution(16830307145957073988)
XLA Ops:
  0.6 0.9 bitcast_dynamic-update-slice_fusion.3
  1.5 0.8 copy-done.4
  2.4 0.7 copy-done.6
  3.1 0.8 copy-done.5
  4.0 1.9 collective-permute-start
  5.9 3.6 collective-permute-start.1
  9.6 1.4 collective-permute-done.1
  11.1 4.2 collective-permute-start.2
  15.3 1.9 collective-permute-start.3
  17.3 6.6 %collective-permute-done.2 = f32[5,2,68,2]{3,2,1,0:T(8,128)S(1)} collective-permute-done((f32[5,2,68,2]{3,2,1,0:T(8,128)S(1)}, f32[5,2,68,2]{3,2,1,0:T(8,128)S(1)}, u32[]{:S(2)}, u32[]{:S(2)}) %collective-permute-start.2) | collective-permute-done | bytes 5472 | tf_op jit(solution)/shard_map/ppermute | solution.py:21
  23.8 6.6 %collective-permute-done.3 = f32[5,2,68,2]{3,2,1,0:T(8,128)S(1)} collective-permute-done((f32[5,2,68,2]{3,2,1,0:T(8,128)S(1)}, f32[5,2,68,2]{3,2,1,0:T(8,128)S(1)}, u32[]{:S(2)}, u32[]{:S(2)}) %collective-permute-start.3) | collective-permute-done | bytes 5472 | tf_op jit(solution)/shard_map/ppermute | solution.py:23
  30.5 0.4 pad_maximum_fusion
  30.9 0.4 fusion.76
  31.4 0.4 multiply_multiply_fusion.1
  31.8 0.3 multiply_multiply_fusion
  32.1 0.5 copy-done.1
  32.9 2.1 collective-permute-start.4
  35.0 3.5 collective-permute-start.5
  38.5 1.3 collective-permute-done.5
  39.9 1.9 collective-permute-start.6
  41.8 6.0 %collective-permute-start.7 = (f32[2,66,1]{2,1,0:T(8,128)S(1)}, f32[2,66,1]{2,1,0:T(8,128)S(1)}, u32[]{:S(2)}, u32[]{:S(2)}) collective-permute-start(f32[2,66,1]{2,1,0:T(8,128)S(1)} %get-tuple-element.39), channel_id=1, source_target_pairs={{0,1},{1,2},{2,3},{3,4},{4,5},{5,6},{6,7},{7,8},{8,9},{9,10},{10,1... | collective-permute-start | bytes 1592 | tf_op jit(solution)/shard_map/ppermute | solution.py:21
  47.8 0.5 collective-permute-done.6
  48.4 1.8 collective-permute-done.7
  50.2 0.3 multiply_reduce_fusion.3
  50.7 106.2 %all-reduce.3 = (f32[1024]{0:T(1024)S(1)}, f32[2]{0:T(128)S(1)}) all-reduce(f32[1024]{0:T(1024)S(1)} %dynamic-update-slice, f32[2]{0:T(128)S(1)} %get-tuple-element.3), channel_id=2, replica_groups=mesh['row'=16,'col'=32] {'row','col'}, use_global_device_ids=true, to_apply=%add | all-reduce | flops 1026 | bytes 8208
  157.5 94.5 %all-reduce.1 = f32[1024]{0:T(1024)S(1)} all-reduce(f32[1024]{0:T(1024)S(1)} %dynamic-update-slice.1), channel_id=3, replica_groups=mesh['row'=16,'col'=32] {'row','col'}, use_global_device_ids=true, to_apply=%add.1 | all-reduce | flops 1024 | bytes 8192
  252.4 1.9 collective-permute-start.8
  254.3 3.6 collective-permute-start.9
  258.0 1.3 collective-permute-done.9
  259.3 2.2 collective-permute-start.10
  261.5 5.8 collective-permute-start.11
  267.3 1.0 collective-permute-done.10
  268.3 1.2 collective-permute-done.11
  269.5 0.3 multiply_reduce_fusion.1
  269.8 100.5 %psum.22 = f32[2]{0:T(128)S(1)} all-reduce(f32[2]{0:T(128)S(1)} %get-tuple-element.7), channel_id=1, replica_groups=mesh['row'=16,'col'=32] {'row','col'}, use_global_device_ids=true, to_apply=%region_7.8 | all-reduce | flops 2 | bytes 16 | tf_op jit(solution)/shard_map/psum | solution.py:140
  370.6 94.5 %all-reduce.2 = f32[1024]{0:T(1024)S(1)} all-reduce(f32[1024]{0:T(1024)S(1)} %dynamic-update-slice.2), channel_id=4, replica_groups=mesh['row'=16,'col'=32] {'row','col'}, use_global_device_ids=true, to_apply=%add.2 | all-reduce | flops 1024 | bytes 8192
  465.5 1.9 collective-permute-start.12
  467.4 3.6 collective-permute-start.13
  471.0 1.3 collective-permute-done.13
  472.4 2.2 collective-permute-start.14
  474.6 5.8 collective-permute-start.15
  480.4 0.8 collective-permute-done.14
  481.2 1.2 collective-permute-done.15
  482.7 100.6 %psum.23 = f32[2]{0:T(128)S(1)} all-reduce(f32[2]{0:T(128)S(1)} %fusion.28), channel_id=1, replica_groups=mesh['row'=16,'col'=32] {'row','col'}, use_global_device_ids=true, to_apply=%region_11.12 | all-reduce | flops 2 | bytes 16 | tf_op jit(solution)/shard_map/psum | solution.py:140
  583.4 1.9 collective-permute-start.17
  585.3 1.9 collective-permute-start.16
  587.4 6.5 %collective-permute-done.16 = f32[2,64,1]{2,1,0:T(8,128)S(1)} collective-permute-done((f32[2,64,1]{2,1,0:T(8,128)S(1)}, f32[2,64,1]{2,1,0:T(8,128)S(1)}, u32[]{:S(2)}, u32[]{:S(2)}) %collective-permute-start.16) | collective-permute-done | bytes 544 | tf_op jit(solution)/shard_map/ppermute | solution.py:33
  593.8 0.8 fusion.21
  (59 shorter events, 3.4 us)
Async XLA Ops:
  0.6 0.9 copy-start.3
  1.5 0.8 copy-start.4
  2.4 0.8 copy-start.6
  3.1 0.8 copy-start.5
  4.0 5.6 collective-permute-start
  5.9 5.0 collective-permute-start.1
  11.1 12.7 %collective-permute-start.2 = (f32[5,2,68,2]{3,2,1,0:T(8,128)S(1)}, f32[5,2,68,2]{3,2,1,0:T(8,128)S(1)}, u32[]{:S(2)}, u32[]{:S(2)}) collective-permute-start(f32[5,2,68,2]{3,2,1,0:T(8,128)S(1)} %get-tuple-element.30), channel_id=1, source_target_pairs={{0,1},{1,2},{2,3},{3,4},{4,5},{5,6},{6,7},{7,8},{8,9},{9,10},{10,1... | collective-permute-start | bytes 16328 | tf_op jit(solution)/shard_map/ppermute | solution.py:21
  15.3 15.1 %collective-permute-start.3 = (f32[5,2,68,2]{3,2,1,0:T(8,128)S(1)}, f32[5,2,68,2]{3,2,1,0:T(8,128)S(1)}, u32[]{:S(2)}, u32[]{:S(2)}) collective-permute-start(f32[5,2,68,2]{3,2,1,0:T(8,128)S(1)} %get-tuple-element.31), channel_id=1, source_target_pairs={{1,0},{2,1},{3,2},{4,3},{5,4},{6,5},{7,6},{8,7},{9,8},{10,9},{11,1... | collective-permute-start | bytes 16328 | tf_op jit(solution)/shard_map/ppermute | solution.py:23
  31.8 0.8 copy-start.1
  31.8 0.9 copy-start.2
  32.9 5.6 collective-permute-start.4
  35.0 4.8 collective-permute-start.5
  39.9 8.5 %collective-permute-start.6 = (f32[2,66,1]{2,1,0:T(8,128)S(1)}, f32[2,66,1]{2,1,0:T(8,128)S(1)}, u32[]{:S(2)}, u32[]{:S(2)}) collective-permute-start(f32[2,66,1]{2,1,0:T(8,128)S(1)} %get-tuple-element.38), channel_id=1, source_target_pairs={{1,0},{2,1},{3,2},{4,3},{5,4},{6,5},{7,6},{8,7},{9,8},{10,9},{11,1... | collective-permute-start | bytes 1592 | tf_op jit(solution)/shard_map/ppermute | solution.py:23
  41.8 8.4 %collective-permute-start.7 = (f32[2,66,1]{2,1,0:T(8,128)S(1)}, f32[2,66,1]{2,1,0:T(8,128)S(1)}, u32[]{:S(2)}, u32[]{:S(2)}) collective-permute-start(f32[2,66,1]{2,1,0:T(8,128)S(1)} %get-tuple-element.39), channel_id=1, source_target_pairs={{0,1},{1,2},{2,3},{3,4},{4,5},{5,6},{6,7},{7,8},{8,9},{9,10},{10,1... | collective-permute-start | bytes 1592 | tf_op jit(solution)/shard_map/ppermute | solution.py:21
  252.4 5.6 collective-permute-start.8
  254.3 4.9 collective-permute-start.9
  259.3 9.0 %collective-permute-start.10 = (f32[2,66,1]{2,1,0:T(8,128)S(1)}, f32[2,66,1]{2,1,0:T(8,128)S(1)}, u32[]{:S(2)}, u32[]{:S(2)}) collective-permute-start(f32[2,66,1]{2,1,0:T(8,128)S(1)} %get-tuple-element.36), channel_id=1, source_target_pairs={{1,0},{2,1},{3,2},{4,3},{5,4},{6,5},{7,6},{8,7},{9,8},{10,9},{11,1... | collective-permute-start | bytes 1592 | tf_op jit(solution)/shard_map/ppermute | solution.py:23
  261.5 8.0 %collective-permute-start.11 = (f32[2,66,1]{2,1,0:T(8,128)S(1)}, f32[2,66,1]{2,1,0:T(8,128)S(1)}, u32[]{:S(2)}, u32[]{:S(2)}) collective-permute-start(f32[2,66,1]{2,1,0:T(8,128)S(1)} %get-tuple-element.37), channel_id=1, source_target_pairs={{0,1},{1,2},{2,3},{3,4},{4,5},{5,6},{6,7},{7,8},{8,9},{9,10},{10,1... | collective-permute-start | bytes 1592 | tf_op jit(solution)/shard_map/ppermute | solution.py:21
  465.5 5.6 collective-permute-start.12
  467.4 4.9 collective-permute-start.13
  472.4 8.8 %collective-permute-start.14 = (f32[2,66,1]{2,1,0:T(8,128)S(1)}, f32[2,66,1]{2,1,0:T(8,128)S(1)}, u32[]{:S(2)}, u32[]{:S(2)}) collective-permute-start(f32[2,66,1]{2,1,0:T(8,128)S(1)} %get-tuple-element.34), channel_id=1, source_target_pairs={{1,0},{2,1},{3,2},{4,3},{5,4},{6,5},{7,6},{8,7},{9,8},{10,9},{11,1... | collective-permute-start | bytes 1592 | tf_op jit(solution)/shard_map/ppermute | solution.py:23
  474.6 7.8 %collective-permute-start.15 = (f32[2,66,1]{2,1,0:T(8,128)S(1)}, f32[2,66,1]{2,1,0:T(8,128)S(1)}, u32[]{:S(2)}, u32[]{:S(2)}) collective-permute-start(f32[2,66,1]{2,1,0:T(8,128)S(1)} %get-tuple-element.35), channel_id=1, source_target_pairs={{0,1},{1,2},{2,3},{3,4},{4,5},{5,6},{6,7},{7,8},{8,9},{9,10},{10,1... | collective-permute-start | bytes 1592 | tf_op jit(solution)/shard_map/ppermute | solution.py:21
  583.4 10.5 %copy-start = (f32[2,64,128]{2,1,0:T(8,128)}, f32[2,64,128]{2,1,0:T(8,128)S(1)}, u32[]{:S(2)}) copy-start(f32[2,64,128]{2,1,0:T(8,128)S(1)} %multiply_add_fusion) | copy-start | bytes 196612
  583.4 10.4 %collective-permute-start.17 = (f32[2,1,128]{2,1,0:T(1,128)S(1)}, f32[2,1,128]{2,1,0:T(1,128)S(1)}, u32[]{:S(2)}, u32[]{:S(2)}) collective-permute-start(f32[2,1,128]{2,1,0:T(1,128)S(1)} %slice.398), channel_id=1, source_target_pairs={{32,0},{64,32},{96,64},{128,96},{160,128},{192,160},{224,192},{256... | collective-permute-start | bytes 3080 | tf_op jit(solution)/shard_map/ppermute | solution.py:33
  585.3 8.5 %collective-permute-start.16 = (f32[2,64,1]{2,1,0:T(8,128)S(1)}, f32[2,64,1]{2,1,0:T(8,128)S(1)}, u32[]{:S(2)}, u32[]{:S(2)}) collective-permute-start(f32[2,64,1]{2,1,0:T(8,128)S(1)} %bitcast.19), channel_id=1, source_target_pairs={{1,0},{2,1},{3,2},{4,3},{5,4},{6,5},{7,6},{8,7},{9,8},{10,9},{11,1... | collective-permute-start | bytes 1544 | tf_op jit(solution)/shard_map/ppermute | solution.py:33
